TPU v7x, 512 devices: a whole 4x8x8 slice. The times are simulated.
512 devices in a mesh: dp: 32 (over y_lo, z), row: 4 (over x), col: 4 (over y_hi, core).
Axes of the slice: x: 4, y: 8 (y_hi: 2, y_lo: 4; y = y_hi * 4 + y_lo), z: 8, core: 2. Of those that a mesh axis runs over, the one named last changes fastest.
Arguments:
- query_out: bfloat16 [6144, 4096], P(('dp', 'row'), 'col'), may hold values from -6 to 6
- query_in: bfloat16 [6144, 4096], P(('dp', 'col')), may hold values from -6 to 6
- out_basis: bfloat16 [4096, 4096], P('col', ('dp', 'row')), may hold values from -0.09375 to 0.09375
- in_basis: bfloat16 [4096, 4096], P(('dp', 'row'), 'col'), may hold values from -0.09375 to 0.09375
- eigvals: float32 [4096, 4096], P(('dp', 'row'), 'col'), may hold values from 16 to 1024
- train_out: bfloat16 [6144, 4096], P(('dp', 'row'), 'col'), may hold values from -0.09375 to 0.09375
- train_in: bfloat16 [6144, 4096], P(('dp', 'col')), may hold values from -0.09375 to 0.09375
Outputs:
- precond: float32 [4096, 4096], P(('dp', 'row'), 'col')
- scores: float32 [6144], P('dp')
All inputs are finite; a program needn't handle non-finite values.
Results may differ from a plain program's by a relative error of at most 0.028.
Values may be sent and summed in bfloat16 or wider, within the bound.
No kernel may reach another device: no remote copies, remote signals or barrier semaphores. Data moves between devices by JAX's collectives and lax.ppermute only.
A program may use at most 64 MiB of HBM per device.

v0:
```python
import jax
import jax.numpy as jnp
from jax import lax
from jax.sharding import PartitionSpec as P

damping = 1.0


def rotate_out(tok_rows, basis_panel):
    gathered = lax.all_gather(tok_rows, "row", axis=0, tiled=True)
    partial_sum = jnp.dot(gathered, basis_panel, preferred_element_type=jnp.float32)
    return lax.psum(partial_sum.astype(jnp.bfloat16), "col")


def rotate_in(tok_rows, basis_panel):
    groups = lax.axis_size("dp")
    row_count = lax.axis_size("row")
    sub_width = tok_rows.shape[1] // (groups * row_count)
    split_rows = tok_rows.reshape(tok_rows.shape[0], groups, row_count, sub_width)
    picked = lax.dynamic_index_in_dim(split_rows, lax.axis_index("row"), 2, keepdims=False)
    picked = picked.reshape(tok_rows.shape[0], groups * sub_width)
    gathered = lax.all_gather(picked, "col", axis=0, tiled=True)
    partial_sum = jnp.dot(gathered, basis_panel, preferred_element_type=jnp.float32)
    return lax.psum(partial_sum.astype(jnp.bfloat16), "row")


def per_device(query_out, query_in, out_basis, in_basis, eigvals, train_out, train_in):
    panel_out = lax.all_gather(out_basis, "dp", axis=1, tiled=True)
    panel_in = lax.all_gather(in_basis, "dp", axis=0, tiled=True)
    query_rot = rotate_out(query_out, panel_out)
    query_inr = rotate_in(query_in, panel_in)
    partial_grad = lax.dot_general(
        query_rot, query_inr, (((0,), (0,)), ((), ())), preferred_element_type=jnp.float32
    )
    rows_own = eigvals.shape[0]
    summed = lax.psum(partial_grad.astype(jnp.bfloat16), "dp").astype(jnp.float32)
    owned = lax.dynamic_slice_in_dim(summed, lax.axis_index("dp") * rows_own, rows_own, 0)
    precond = owned / (eigvals + damping)
    shared = precond.astype(jnp.bfloat16)
    train_rot = rotate_out(train_out, panel_out)
    train_inr = rotate_in(train_in, panel_in)
    mixed = jnp.dot(
        train_rot,
        lax.all_gather(shared, "dp", axis=0, tiled=True),
        preferred_element_type=jnp.float32,
    )
    partial_scores = jnp.sum(mixed * train_inr.astype(jnp.float32), axis=1)
    scores = lax.psum(partial_scores, ("row", "col"))
    return (precond, scores)


def solution(mesh):
    in_specs = (
        P(("dp", "row"), "col"),
        P(("dp", "col"), None),
        P("col", ("dp", "row")),
        P(("dp", "row"), "col"),
        P(("dp", "row"), "col"),
        P(("dp", "row"), "col"),
        P(("dp", "col"), None),
    )
    out_specs = (P(("dp", "row"), "col"), P("dp"))
    return jax.shard_map(
        per_device, mesh=mesh, in_specs=in_specs, out_specs=out_specs, check_vma=False
    )
```

profile of v0, /device:TPU:1, one launch (start us, length us, event | category | flops | bytes accessed | tf_op | source)
XLA Modules:
  0.0 969.9 jit_solution(9535577205798143316)
XLA Ops:
  7.2 0.7 all-gather.6.cloned.1.call-update
  7.9 0.7 all-gather.4.cloned.1.call-update
  8.7 1.5 copy.9
  10.2 1.5 copy.11
  11.7 0.1 copy.14
  11.8 0.1 copy.13
  12.0 16.7 %all_gather.27 = bf16[192,1024]{1,0:T(8,128)(2,1)S(1)} all-gather(bf16[48,1024]{1,0:T(8,128)(2,1)S(1)} %copy.14), channel_id=1, replica_groups=mesh['dp'=32,'row'=4,'col'=4] {'col'}, dimensions={0}, use_global_device_ids=true | all-gather | bytes 491520 | tf_op jit(solution)/shard_map/all_gather | solution.py:22
  28.7 12.9 %all_gather.23 = bf16[192,1024]{1,0:T(8,128)(2,1)S(1)} all-gather(bf16[48,1024]{1,0:T(8,128)(2,1)S(1)} %copy.13), channel_id=1, replica_groups=mesh['dp'=32,'row'=4,'col'=4] {'col'}, dimensions={0}, use_global_device_ids=true | all-gather | bytes 491520 | tf_op jit(solution)/shard_map/all_gather | solution.py:22
  41.6 106.6 %all-gather.6.cloned.1.call-done = bf16[1024,1024]{1,0:T(8,128)(2,1)} async-done(((bf16[32,1024]{1,0:T(8,128)(2,1)}), bf16[1024,1024]{1,0:T(8,128)(2,1)}) %all-gather.6.cloned.1.call-update) | async-done | bytes 2097168 | tf_op jit(solution)/shard_map/all_gather | solution.py:29
  148.2 3.1 convolution_convert_fusion.1
  151.3 1.4 convolution_convert_fusion.3
  152.8 10.9 %all_gather.25 = bf16[192,1024]{1,0:T(8,128)(2,1)S(1)} all-gather(bf16[48,1024]{1,0:T(8,128)(2,1)S(1)} %copy-done.3), channel_id=1, replica_groups=mesh['dp'=32,'row'=4,'col'=4] {'row'}, dimensions={0}, use_global_device_ids=true | all-gather | bytes 491520 | tf_op jit(solution)/shard_map/all_gather | solution.py:10
  163.6 10.0 %all_gather.21 = bf16[192,1024]{1,0:T(8,128)(2,1)S(1)} all-gather(bf16[48,1024]{1,0:T(8,128)(2,1)S(1)} %copy-done.4), channel_id=1, replica_groups=mesh['dp'=32,'row'=4,'col'=4] {'row'}, dimensions={0}, use_global_device_ids=true | all-gather | bytes 491520 | tf_op jit(solution)/shard_map/all_gather | solution.py:10
  173.6 126.9 %all-gather.4.cloned.1.call-done = bf16[1024,1024]{0,1:T(8,128)(2,1)} async-done(((bf16[1024,32]{0,1:T(8,128)(2,1)}), bf16[1024,1024]{0,1:T(8,128)(2,1)}) %all-gather.4.cloned.1.call-update) | async-done | bytes 2097168 | tf_op jit(solution)/shard_map/all_gather | solution.py:28
  300.6 3.3 convolution_convert_fusion.2
  303.9 1.6 convolution_convert_fusion.4
  305.6 68.1 %all-reduce.10.cloned.1.call-done = (bf16[192,1024]{1,0:T(8,128)(2,1)}, bf16[192,1024]{1,0:T(8,128)(2,1)}) async-done(((bf16[192,1024]{1,0:T(8,128)(2,1)}, bf16[192,1024]{1,0:T(8,128)(2,1)}), (bf16[192,1024]{1,0:T(8,128)(2,1)}, bf16[192,1024]{1,0:T(8,128)(2,1)})) %all-reduce.10.cloned.1.call-update) | async-done | bytes 786448 | tf_op jit(solution)/shard_map/psum | solution.py:24
  373.7 75.0 %all-reduce.8.cloned.1.call-done = (bf16[192,1024]{1,0:T(8,128)(2,1)}, bf16[192,1024]{1,0:T(8,128)(2,1)}) async-done(((bf16[192,1024]{1,0:T(8,128)(2,1)}, bf16[192,1024]{1,0:T(8,128)(2,1)}), (bf16[192,1024]{1,0:T(8,128)(2,1)}, bf16[192,1024]{1,0:T(8,128)(2,1)})) %all-reduce.8.cloned.1.call-update) | async-done | bytes 786448 | tf_op jit(solution)/shard_map/psum | solution.py:12
  448.7 3.3 convolution_convert_fusion
  452.0 290.8 %all-reduce.6.cloned.1.call-done = bf16[1024,1024]{1,0:T(8,128)(2,1)} async-done(((bf16[1024,1024]{1,0:T(8,128)(2,1)}), bf16[1024,1024]{1,0:T(8,128)(2,1)}) %all-reduce.6.cloned.1.call-update) | async-done | bytes 2097168 | tf_op jit(solution)/shard_map/psum | solution.py:36
  742.8 1.5 fusion.1
  744.4 150.6 %all-gather.8.cloned.1.call-done = bf16[1024,1024]{1,0:T(8,128)(2,1)} async-done(((bf16[32,1024]{1,0:T(8,128)(2,1)}), bf16[1024,1024]{1,0:T(8,128)(2,1)}) %all-gather.8.cloned.1.call-update) | async-done | bytes 2097168 | tf_op jit(solution)/shard_map/all_gather | solution.py:44
  895.0 2.3 fusion
  897.2 65.8 %psum.47 = f32[192]{0:T(256)} all-reduce(f32[192]{0:T(256)S(1)} %fusion), channel_id=1, replica_groups=mesh['dp'=32,'row'=4,'col'=4] {'row','col'}, use_global_device_ids=true, to_apply=%region_6.7 | all-reduce | flops 192 | bytes 1536 | tf_op jit(solution)/shard_map/psum | solution.py:48
  (25 shorter events, 0.4 us)
Async XLA Ops:
  7.2 141.1 %all-gather.6.cloned.1.call-start = ((), (), s32[]{:S(2)}) async-start(), calls=%async_computation.1 | async-start | bytes 2162688 | tf_op jit(solution)/shard_map/all_gather | solution.py:29
  7.9 292.7 %all-gather.4.cloned.1.call-start = ((), (), s32[]{:S(2)}) async-start(), calls=%async_computation | async-start | bytes 2162688 | tf_op jit(solution)/shard_map/all_gather | solution.py:28
  8.6 365.1 %all-reduce.10.cloned.1.call-start = ((), (), s32[]{:S(2)}) async-start(), calls=%async_computation.5 | async-start | bytes 1572864 | tf_op jit(solution)/shard_map/psum | solution.py:24
  148.2 3.1 copy-start.1
  151.3 1.4 copy-start.3
  151.3 12.3 %copy-start.4 = (bf16[48,1024]{1,0:T(8,128)(2,1)S(1)}, bf16[48,1024]{1,0:T(8,128)(2,1)}, u32[]{:S(2)}) copy-start(bf16[48,1024]{1,0:T(8,128)(2,1)} %param.7) | copy-start | bytes 294916
  152.7 295.9 %all-reduce.8.cloned.1.call-start = ((), (), s32[]{:S(2)}) async-start(), calls=%async_computation.4 | async-start | bytes 1572864 | tf_op jit(solution)/shard_map/psum | solution.py:12
  300.6 3.3 copy-start
  305.5 437.3 %all-reduce.6.cloned.1.call-start = ((), (), s32[]{:S(2)}) async-start(), calls=%async_computation.2 | async-start | bytes 4194304 | tf_op jit(solution)/shard_map/psum | solution.py:36
  448.7 294.2 %copy-start.2 = (f32[32,1024]{1,0:T(8,128)S(1)}, f32[32,1024]{1,0:T(8,128)}, u32[]{:S(2)}) copy-start(f32[32,1024]{1,0:T(8,128)} %param.11) | copy-start | bytes 393220
  448.7 446.3 %copy-start.5 = (bf16[192,1024]{1,0:T(8,128)(2,1)S(1)}, bf16[192,1024]{1,0:T(8,128)(2,1)}, u32[]{:S(2)}) copy-start(bf16[192,1024]{1,0:T(8,128)(2,1)} %get-tuple-element.5) | copy-start | bytes 1179652
  448.7 446.3 %copy-start.6 = (bf16[192,1024]{1,0:T(8,128)(2,1)S(1)}, bf16[192,1024]{1,0:T(8,128)(2,1)}, u32[]{:S(2)}) copy-start(bf16[192,1024]{1,0:T(8,128)(2,1)} %get-tuple-element.3) | copy-start | bytes 1179652
  452.0 443.0 %all-gather.8.cloned.1.call-start = ((), (), s32[]{:S(2)}) async-start(), calls=%async_computation.3 | async-start | bytes 2162688 | tf_op jit(solution)/shard_map/all_gather | solution.py:44
Sparse Core Ops, SparseCore 0:
  10.0 138.1 all-gather.5
  150.3 150.2 all-gather.3
  303.0 70.6 all-reduce.9
  376.6 72.0 all-reduce.7
  452.1 290.6 all-reduce.5
  744.7 150.1 all-gather.7
where the time goes:
time: 970 us
  waiting for transfers between devices  819 us (84%)
  blocking collectives  116 us (12%)
  matrix products  14.9 us (2%)
  between operations  14.2 us (1%)
    psum x1, waiting for transfers between devices, per_device(): lax.psum(partial_grad.astype(jnp.bfloat16), 'dp').astype(jnp.float32)  291 us
    all_gather x1, waiting for transfers between devices, per_device(): lax.all_gather(shared, 'dp', axis=0, tiled=True)  151 us
    all_gather x1, waiting for transfers between devices, per_device(): panel_out = lax.all_gather(out_basis, 'dp', axis=1, tiled=True)  127 us
    all_gather x1, waiting for transfers between devices, per_device(): panel_in = lax.all_gather(in_basis, 'dp', axis=0, tiled=True)  107 us
    psum x1, waiting for transfers between devices, rotate_out(): return lax.psum(partial_sum.astype(jnp.bfloat16), 'col')  75 us
    psum x1, waiting for transfers between devices, rotate_in(): return lax.psum(partial_sum.astype(jnp.bfloat16), 'row')  68.1 us
    psum x1, blocking collectives, per_device(): scores = lax.psum(partial_scores, ('row', 'col'))  65.8 us
    all_gather x2, blocking collectives, rotate_in(): gathered = lax.all_gather(picked, 'col', axis=0, tiled=True)  29.6 us
  transfers between devices with their start and end apart: 6, of which 6 were waited for; matrix products, arithmetic and copies ran while one was open for 1% of the time, Pallas kernels for 0%

commit v1 on v0

--- a/solution.py
+++ b/solution.py
@@ -7,7 +7,33 @@
 
 
 def rotate_out(tok_rows, basis_panel):
-    gathered = lax.all_gather(tok_rows, "row", axis=0, tiled=True)
+    latest, far_arr, local_next = (lax.psum(1, "row"), lax.axis_index("row"), tok_rows.shape[0])
+    gathered = lax.dynamic_update_slice_in_dim(
+        jnp.zeros(
+            tuple(
+                (hop_no * latest if u == 0 else hop_no for u, hop_no in enumerate(tok_rows.shape))
+            ),
+            tok_rows.dtype,
+        ),
+        tok_rows,
+        far_arr * local_next,
+        axis=0,
+    )
+    part_now = parts_out = tok_rows
+    for idx in range(1, latest // 2 + 1):
+        part_now = lax.ppermute(
+            part_now, "row", tuple(((u, (u + 1) % latest) for u in range(latest)))
+        )
+        gathered = lax.dynamic_update_slice_in_dim(
+            gathered, part_now, (far_arr - idx) % latest * local_next, axis=0
+        )
+        if 2 * idx < latest:
+            parts_out = lax.ppermute(
+                parts_out, "row", tuple(((u, (u - 1) % latest) for u in range(latest)))
+            )
+            gathered = lax.dynamic_update_slice_in_dim(
+                gathered, parts_out, (far_arr + idx) % latest * local_next, axis=0
+            )
     partial_sum = jnp.dot(gathered, basis_panel, preferred_element_type=jnp.float32)
     return lax.psum(partial_sum.astype(jnp.bfloat16), "col")
 

time: 970 us -> 971 us (level)
  starting transfers between devices: 0.24 us -> 17.9 us
  waiting for transfers between devices: 819 us -> 809 us
    all_gather x2 -> x0, blocking collectives: 20.9 us -> none  [rotate_out(): gathered = lax.all_gather(tok_rows, 'row', axis=0, tiled=True)]
    ppermute x0 -> x6, starting transfers between devices: none -> 17.6 us  [the longest x4 10 us: rotate_out(): lax.ppermute(part_now, 'row', tuple(((u, (u + 1) % latest) for u in range...]
    all_gather x2, blocking collectives: 29.6 us -> 44.2 us  [rotate_in(): gathered = lax.all_gather(picked, 'col', axis=0, tiled=True)]
    psum x1, waiting for transfers between devices: 68.1 us -> 53.7 us  [rotate_in(): return lax.psum(partial_sum.astype(jnp.bfloat16), 'row')]
    all_gather x1, waiting for transfers between devices: 127 us -> 114 us  [per_device(): panel_out = lax.all_gather(out_basis, 'dp', axis=1, tiled=True)]
    psum x1, waiting for transfers between devices: 75 us -> 84.8 us  [rotate_out(): return lax.psum(partial_sum.astype(jnp.bfloat16), 'col')]
  transfers between devices with their start and end apart: 6 -> 12, of which waited for: 6 -> 8; matrix products, arithmetic and copies ran while one was open for 1% -> 1% of each run, Pallas kernels for 0% -> 0%
where the time goes in v1:
time: 971 us
  waiting for transfers between devices  809 us (83%)
  blocking collectives  110 us (11%)
  starting transfers between devices  17.9 us (2%)
  matrix products  14.9 us (2%)
  between operations  14.4 us (1%)
    psum x1, waiting for transfers between devices, per_device(): lax.psum(partial_grad.astype(jnp.bfloat16), 'dp').astype(jnp.float32)  295 us
    all_gather x1, waiting for transfers between devices, per_device(): lax.all_gather(shared, 'dp', axis=0, tiled=True)  151 us
    all_gather x1, waiting for transfers between devices, per_device(): panel_out = lax.all_gather(out_basis, 'dp', axis=1, tiled=True)  114 us
    all_gather x1, waiting for transfers between devices, per_device(): panel_in = lax.all_gather(in_basis, 'dp', axis=0, tiled=True)  105 us
    psum x1, waiting for transfers between devices, rotate_out(): return lax.psum(partial_sum.astype(jnp.bfloat16), 'col')  84.8 us
    psum x1, blocking collectives, per_device(): scores = lax.psum(partial_scores, ('row', 'col'))  65.8 us
    psum x1, waiting for transfers between devices, rotate_in(): return lax.psum(partial_sum.astype(jnp.bfloat16), 'row')  53.7 us
    all_gather x2, blocking collectives, rotate_in(): gathered = lax.all_gather(picked, 'col', axis=0, tiled=True)  44.2 us
  transfers between devices with their start and end apart: 12, of which 8 were waited for; matrix products, arithmetic and copies ran while one was open for 1% of the time, Pallas kernels for 0%

profile of v1, /device:TPU:1, one launch (start us, length us, event | category | flops | bytes accessed | tf_op | source)
XLA Modules:
  0.0 971.0 jit_solution(11326834924682512442)
XLA Ops:
  8.7 3.9 collective-permute-start.3
  12.6 3.2 collective-permute-start.4
  15.8 2.1 collective-permute-start
  17.9 4.4 collective-permute-start.1
  23.9 1.5 copy.11
  25.8 1.9 collective-permute-start.5
  27.8 2.1 collective-permute-start.2
  30.0 2.4 collective-permute-done.5
  32.4 1.9 collective-permute-done.2
  34.3 113.8 %all-gather.4.cloned.1.call-done = bf16[1024,1024]{0,1:T(8,128)(2,1)} async-done(((bf16[1024,32]{0,1:T(8,128)(2,1)}), bf16[1024,1024]{0,1:T(8,128)(2,1)}) %all-gather.4.cloned.1.call-update) | async-done | bytes 2097168 | tf_op jit(solution)/shard_map/all_gather | solution.py:54
  148.2 3.4 convolution_convert_fusion.2
  151.5 1.6 convolution_convert_fusion.4
  153.3 33.0 %all_gather.19 = bf16[192,1024]{1,0:T(8,128)(2,1)S(1)} all-gather(bf16[48,1024]{1,0:T(8,128)(2,1)S(1)} %copy.14), channel_id=1, replica_groups=mesh['dp'=32,'row'=4,'col'=4] {'col'}, dimensions={0}, use_global_device_ids=true | all-gather | bytes 491520 | tf_op jit(solution)/shard_map/all_gather | solution.py:48
  186.4 11.2 %all_gather.16 = bf16[192,1024]{1,0:T(8,128)(2,1)S(1)} all-gather(bf16[48,1024]{1,0:T(8,128)(2,1)S(1)} %copy.13), channel_id=1, replica_groups=mesh['dp'=32,'row'=4,'col'=4] {'col'}, dimensions={0}, use_global_device_ids=true | all-gather | bytes 491520 | tf_op jit(solution)/shard_map/all_gather | solution.py:48
  197.6 104.6 %all-gather.6.cloned.1.call-done = bf16[1024,1024]{1,0:T(8,128)(2,1)} async-done(((bf16[32,1024]{1,0:T(8,128)(2,1)}), bf16[1024,1024]{1,0:T(8,128)(2,1)}) %all-gather.6.cloned.1.call-update) | async-done | bytes 2097168 | tf_op jit(solution)/shard_map/all_gather | solution.py:55
  302.2 3.1 convolution_convert_fusion.1
  306.7 84.8 %all-reduce.8.cloned.1.call-done = (bf16[192,1024]{1,0:T(8,128)(2,1)}, bf16[192,1024]{1,0:T(8,128)(2,1)}) async-done(((bf16[192,1024]{1,0:T(8,128)(2,1)}, bf16[192,1024]{1,0:T(8,128)(2,1)}), (bf16[192,1024]{1,0:T(8,128)(2,1)}, bf16[192,1024]{1,0:T(8,128)(2,1)})) %all-reduce.8.cloned.1.call-update) | async-done | bytes 786448 | tf_op jit(solution)/shard_map/psum | solution.py:38
  391.5 53.7 %all-reduce.10.cloned.1.call-done = (bf16[192,1024]{1,0:T(8,128)(2,1)}, bf16[192,1024]{1,0:T(8,128)(2,1)}) async-done(((bf16[192,1024]{1,0:T(8,128)(2,1)}, bf16[192,1024]{1,0:T(8,128)(2,1)}), (bf16[192,1024]{1,0:T(8,128)(2,1)}, bf16[192,1024]{1,0:T(8,128)(2,1)})) %all-reduce.10.cloned.1.call-update) | async-done | bytes 786448 | tf_op jit(solution)/shard_map/psum | solution.py:50
  445.2 3.3 convolution_convert_fusion
  448.6 295.3 %all-reduce.6.cloned.1.call-done = bf16[1024,1024]{1,0:T(8,128)(2,1)} async-done(((bf16[1024,1024]{1,0:T(8,128)(2,1)}), bf16[1024,1024]{1,0:T(8,128)(2,1)}) %all-reduce.6.cloned.1.call-update) | async-done | bytes 2097168 | tf_op jit(solution)/shard_map/psum | solution.py:62
  743.9 1.5 fusion.1
  745.4 150.6 %all-gather.8.cloned.1.call-done = bf16[1024,1024]{1,0:T(8,128)(2,1)} async-done(((bf16[32,1024]{1,0:T(8,128)(2,1)}), bf16[1024,1024]{1,0:T(8,128)(2,1)}) %all-gather.8.cloned.1.call-update) | async-done | bytes 2097168 | tf_op jit(solution)/shard_map/all_gather | solution.py:70
  896.0 2.3 fusion
  898.3 65.8 %psum.47 = f32[192]{0:T(256)} all-reduce(f32[192]{0:T(256)S(1)} %fusion), channel_id=1, replica_groups=mesh['dp'=32,'row'=4,'col'=4] {'row','col'}, use_global_device_ids=true, to_apply=%region_6.7 | all-reduce | flops 192 | bytes 1536 | tf_op jit(solution)/shard_map/psum | solution.py:74
  (45 shorter events, 5.0 us)
Async XLA Ops:
  7.2 141.0 %all-gather.4.cloned.1.call-start = ((), (), s32[]{:S(2)}) async-start(), calls=%async_computation | async-start | bytes 2162688 | tf_op jit(solution)/shard_map/all_gather | solution.py:54
  7.9 294.3 %all-gather.6.cloned.1.call-start = ((), (), s32[]{:S(2)}) async-start(), calls=%async_computation.1 | async-start | bytes 2162688 | tf_op jit(solution)/shard_map/all_gather | solution.py:55
  8.6 382.8 %all-reduce.8.cloned.1.call-start = ((), (), s32[]{:S(2)}) async-start(), calls=%async_computation.4 | async-start | bytes 1572864 | tf_op jit(solution)/shard_map/psum | solution.py:38
  8.7 17.1 %collective-permute-start.3 = (bf16[48,1024]{1,0:T(8,128)(2,1)}, bf16[48,1024]{1,0:T(8,128)(2,1)S(1)}, u32[]{:S(2)}, u32[]{:S(2)}) collective-permute-start(bf16[48,1024]{1,0:T(8,128)(2,1)} %param.12), channel_id=1, source_target_pairs={{0,4},{4,8},{8,12},{12,0},{1,5},{5,9},{9,13},{13,1},{2,6},{6,10},{... | collective-permute-start | bytes 294920 | tf_op jit(solution)/shard_map/ppermute | solution.py:24
  12.6 17.3 %collective-permute-start.4 = (bf16[48,1024]{1,0:T(8,128)(2,1)}, bf16[48,1024]{1,0:T(8,128)(2,1)S(1)}, u32[]{:S(2)}, u32[]{:S(2)}) collective-permute-start(bf16[48,1024]{1,0:T(8,128)(2,1)} %param.12), channel_id=1, source_target_pairs={{0,12},{4,0},{8,4},{12,8},{1,13},{5,1},{9,5},{13,9},{2,14},{6,2},{... | collective-permute-start | bytes 294920 | tf_op jit(solution)/shard_map/ppermute | solution.py:31
  15.8 11.9 %collective-permute-start = (bf16[48,1024]{1,0:T(8,128)(2,1)}, bf16[48,1024]{1,0:T(8,128)(2,1)S(1)}, u32[]{:S(2)}, u32[]{:S(2)}) collective-permute-start(bf16[48,1024]{1,0:T(8,128)(2,1)} %param.7), channel_id=1, source_target_pairs={{0,4},{4,8},{8,12},{12,0},{1,5},{5,9},{9,13},{13,1},{2,6},{6,10},{... | collective-permute-start | bytes 294920 | tf_op jit(solution)/shard_map/ppermute | solution.py:24
  17.9 12.0 %collective-permute-start.1 = (bf16[48,1024]{1,0:T(8,128)(2,1)}, bf16[48,1024]{1,0:T(8,128)(2,1)S(1)}, u32[]{:S(2)}, u32[]{:S(2)}) collective-permute-start(bf16[48,1024]{1,0:T(8,128)(2,1)} %param.7), channel_id=1, source_target_pairs={{0,12},{4,0},{8,4},{12,8},{1,13},{5,1},{9,5},{13,9},{2,14},{6,2},{... | collective-permute-start | bytes 294920 | tf_op jit(solution)/shard_map/ppermute | solution.py:31
  22.4 3.3 copy-start.3
  23.9 1.8 copy-start.4
  25.8 6.6 collective-permute-start.5
  27.8 6.6 collective-permute-start.2
  148.2 3.4 copy-start.1
  153.2 292.0 %all-reduce.10.cloned.1.call-start = ((), (), s32[]{:S(2)}) async-start(), calls=%async_computation.5 | async-start | bytes 1572864 | tf_op jit(solution)/shard_map/psum | solution.py:50
  302.2 3.1 copy-start
  306.7 437.2 %all-reduce.6.cloned.1.call-start = ((), (), s32[]{:S(2)}) async-start(), calls=%async_computation.2 | async-start | bytes 4194304 | tf_op jit(solution)/shard_map/psum | solution.py:62
  445.2 298.6 %copy-start.2 = (f32[32,1024]{1,0:T(8,128)S(1)}, f32[32,1024]{1,0:T(8,128)}, u32[]{:S(2)}) copy-start(f32[32,1024]{1,0:T(8,128)} %param.11) | copy-start | bytes 393220
  445.2 450.8 %copy-start.5 = (bf16[192,1024]{1,0:T(8,128)(2,1)S(1)}, bf16[192,1024]{1,0:T(8,128)(2,1)}, u32[]{:S(2)}) copy-start(bf16[192,1024]{1,0:T(8,128)(2,1)} %get-tuple-element.3) | copy-start | bytes 1179652
  445.2 450.8 %copy-start.6 = (bf16[192,1024]{1,0:T(8,128)(2,1)S(1)}, bf16[192,1024]{1,0:T(8,128)(2,1)}, u32[]{:S(2)}) copy-start(bf16[192,1024]{1,0:T(8,128)(2,1)} %get-tuple-element.5) | copy-start | bytes 1179652
  448.5 447.5 %all-gather.8.cloned.1.call-start = ((), (), s32[]{:S(2)}) async-start(), calls=%async_computation.3 | async-start | bytes 2162688 | tf_op jit(solution)/shard_map/all_gather | solution.py:70
Sparse Core Ops, SparseCore 0:
  10.1 138.0 all-gather.3
  150.3 151.9 all-gather.5
  305.2 86.2 all-reduce.7
  393.7 51.4 all-reduce.9
  448.6 295.1 all-reduce.5
  745.8 150.1 all-gather.7
